TPU v7x, 32 devices: a whole 2x2x4 slice. The times are simulated.
32 devices in a mesh: row: 8 (over y, x, core), col: 4 (over z).
Axes of the slice: x: 2, y: 2, z: 4, core: 2. Of those that a mesh axis runs over, the one named last changes fastest.
Arguments:
- covariance: float32 [4096, 2, 2048], P('row', None, 'col'), may hold values from 0 to 1.1, as said below
- diag_inverse: float32 [512, 512], replicated, as said below
Outputs:
- panels: float32 [4096, 1024], P('row', 'col')
- trailing: float32 [4096, 2, 2048], P('row', None, 'col')
Inputs may be any that keep to these rules, and one draw needn't show every extreme that they name: `covariance`: K is symmetric and positive definite, its smallest eigenvalue 0.1 or more. `diag_inverse`: the inverse of the lower Cholesky factor of K[0:512, 0:512].
All inputs are finite; a program needn't handle non-finite values.
Results may differ from a plain program's by a relative error of at most 0.0003.
Values sent between devices are 32-bit elements; how exact they have to be, the bound alone decides.
No kernel may reach another device: no remote copies, remote signals or barrier semaphores. Data moves between devices by JAX's collectives and lax.ppermute only.
A program may use at most 128 MiB of HBM per device.

v0:
```python
import jax
import jax.numpy as jnp
from jax import lax
from jax.sharding import PartitionSpec as P

highest = lax.Precision.HIGHEST


def broadcast(array, axis, root):
    mine = lax.axis_index(axis) == root
    return lax.psum(jnp.where(mine, array, jnp.zeros_like(array)), axis)


def outer_product(left, right):
    return lax.dot_general(
        left, right, (((1,), (1,)), ((), ())), precision=highest, preferred_element_type=jnp.float32
    )


def local(covariance, diag_inverse):
    tile_size = covariance.shape[0]
    row_index = lax.axis_index("row")
    col_index = lax.axis_index("col")
    col_count = lax.axis_size("col")
    cycles = lax.axis_size("row") // col_count
    columns = [position * col_count + col_index for position in range(cycles)]
    block_tiles = [covariance[:, position, :] for position in range(cycles)]
    zero_tile = jnp.zeros((tile_size, tile_size), jnp.float32)
    local_first = lax.cond(
        col_index == 0, lambda: outer_product(block_tiles[0], diag_inverse), lambda: zero_tile
    )
    own_first = broadcast(local_first, "col", 0)
    slot_tiles = jnp.stack([jnp.where(row_index == column, own_first, 0.0) for column in columns])
    summed_first = lax.psum(slot_tiles, "row")
    remote_first = [summed_first[position] for position in range(cycles)]

    def lower_update(current, own_panel, remote_panel, column, first_col):
        keep_mask = (row_index >= column) & (column >= first_col)
        return lax.cond(
            keep_mask, lambda: current - outer_product(own_panel, remote_panel), lambda: current
        )

    block_tiles = [
        lower_update(block_tiles[position], own_first, remote_first[position], columns[position], 1)
        for position in range(cycles)
    ]
    is_owner = (row_index == 1) & (col_index == 1)
    identity = jnp.eye(tile_size, dtype=jnp.float32)
    factor_local = jnp.linalg.cholesky(jnp.where(is_owner, block_tiles[0], identity))
    factor = broadcast(factor_local, "row", 1)

    def solve_panel():
        solved = jax.scipy.linalg.solve_triangular(factor, block_tiles[0].T, lower=True).T
        return jnp.where(row_index >= 1, solved, 0.0)

    local_second = lax.cond(col_index == 1, solve_panel, lambda: zero_tile)
    own_second = broadcast(local_second, "col", 1)
    slot_second = jnp.stack([jnp.where(row_index == column, own_second, 0.0) for column in columns])
    summed_second = lax.psum(slot_second, "row")
    remote_second = [summed_second[position] for position in range(cycles)]
    block_tiles = [
        lower_update(
            block_tiles[position], own_second, remote_second[position], columns[position], 2
        )
        for position in range(cycles)
    ]
    finals = [
        jnp.where(
            (row_index >= columns[position]) & (columns[position] >= 2), block_tiles[position], 0.0
        )
        for position in range(cycles)
    ]
    trailing = jnp.stack(finals, axis=1)
    both_panels = jnp.concatenate([own_first, own_second], axis=1)
    share_width = both_panels.shape[1] // col_count
    panels = lax.dynamic_slice_in_dim(both_panels, col_index * share_width, share_width, 1)
    return (panels, trailing)


def solution(mesh):
    return jax.shard_map(
        local,
        mesh=mesh,
        in_specs=(P("row", None, "col"), P()),
        out_specs=(P("row", "col"), P("row", None, "col")),
        check_vma=False,
    )
```

profile of v0, /device:TPU:22, one launch (start us, length us, event | category | flops | bytes accessed | tf_op | source)
XLA Modules:
  0.0 480.6 jit_solution(18360229636380562185)
XLA Ops:
  7.2 5.0 %fusion.42 = (f32[512,1,512]{2,1,0:T(1,128)}, f32[512,1,512]{2,1,0:T(1,128)S(1)}) fusion(f32[512,2,512]{2,1,0:T(2,128)} %param.14), kind=kLoop, calls=%fused_computation.100 | loop fusion | bytes 4194304 | tf_op jit(solution)/shard_map/slice | solution.py:27
  12.3 1.2 copy-done.5
  13.6 1.1 broadcast_select_fusion.1
  14.7 52.3 %all-reduce.7.cloned.1.call-done = f32[512,512]{1,0:T(8,128)} async-done(((f32[512,512]{1,0:T(8,128)}), f32[512,512]{1,0:T(8,128)}) %all-reduce.7.cloned.1.call-update) | async-done | bytes 1048592 | tf_op jit(solution)/shard_map/psum | solution.py:11
  67.0 1.4 select_bitcast_fusion.5
  68.4 1.5 pad_maximum_fusion
  70.0 60.8 %all-reduce.9.cloned.1.call-done = f32[2,512,512]{2,1,0:T(8,128)} async-done(((f32[2,512,512]{2,1,0:T(8,128)}), f32[2,512,512]{2,1,0:T(8,128)}) %all-reduce.9.cloned.1.call-update) | async-done | bytes 2097168 | tf_op jit(solution)/shard_map/psum | solution.py:34
  130.8 3.9 conditional.7
  130.8 3.4 convolution_subtract_fusion
  135.0 1.1 convert_select_fusion
  136.1 2.5 copy.7
  138.7 1.5 fusion.28
  140.1 1.0 copy-done.4
  141.1 11.7 %cholesky.103 = f32[128,128]{1,0:T(8,128)S(1)} custom-call(f32[128,128]{1,0:T(8,128)S(1)} %cholesky.263), custom_call_target="Cholesky" | custom-call | tf_op jit(solution)/shard_map/jit(cholesky)/cholesky | solution.py:49
  152.9 9.8 %custom-call.31 = f32[1,128,128]{1,2,0:T(8,128)S(1)} custom-call(f32[1,128,128]{2,1,0:T(8,128)S(1)} %get-tuple-element.121), custom_call_target="InvertDiagBlocksLowerTriangular" | custom-call | tf_op jit(solution)/shard_map/jit(cholesky)/cholesky | solution.py:49
  162.8 1.2 constant_dynamic-update-slice_fusion.1
  164.0 1.3 convolution_subtract_fusion.7
  165.3 11.7 %cholesky.215 = f32[128,128]{1,0:T(8,128)S(1)} custom-call(f32[128,128]{1,0:T(8,128)S(1)} %cholesky.267), custom_call_target="Cholesky" | custom-call | tf_op jit(solution)/shard_map/jit(cholesky)/cholesky | solution.py:49
  177.1 10.0 %custom-call.32 = f32[1,128,128]{1,2,0:T(8,128)S(1)} custom-call(f32[1,128,128]{2,1,0:T(8,128)S(1)} %get-tuple-element.118), custom_call_target="InvertDiagBlocksLowerTriangular" | custom-call | tf_op jit(solution)/shard_map/jit(cholesky)/cholesky | solution.py:49
  187.3 1.3 convolution_subtract_fusion.8
  188.6 11.7 %cholesky.236 = f32[128,128]{1,0:T(8,128)S(1)} custom-call(f32[128,128]{1,0:T(8,128)S(1)} %cholesky.272), custom_call_target="Cholesky" | custom-call | tf_op jit(solution)/shard_map/jit(cholesky)/cholesky | solution.py:49
  200.4 0.6 compare_reduce_fusion.1
  201.0 9.8 %custom-call.33 = f32[1,128,128]{1,2,0:T(8,128)S(1)} custom-call(f32[1,128,128]{2,1,0:T(8,128)S(1)} %get-tuple-element.115), custom_call_target="InvertDiagBlocksLowerTriangular" | custom-call | tf_op jit(solution)/shard_map/jit(cholesky)/cholesky | solution.py:49
  211.0 1.2 convolution_subtract_fusion.9
  212.3 11.9 %cholesky.253 = f32[128,128]{1,0:T(8,128)S(1)} custom-call(f32[128,128]{1,0:T(8,128)S(1)} %convolution_subtract_fusion.9), custom_call_target="Cholesky" | custom-call | tf_op jit(solution)/shard_map/jit(cholesky)/cholesky | solution.py:49
  224.2 0.7 compare_reduce_fusion
  224.9 0.6 compare_reduce_fusion.2
  228.1 1.1 select_select_fusion
  229.3 56.1 %all-reduce.11.cloned.1.call-done = f32[512,512]{1,0:T(8,128)} async-done(((f32[512,512]{1,0:T(8,128)}), f32[512,512]{1,0:T(8,128)}) %all-reduce.11.cloned.1.call-update) | async-done | bytes 1048592 | tf_op jit(solution)/shard_map/psum | solution.py:11
  285.4 1.1 conditional.8
  285.4 1.1 broadcast.194.clone
  286.5 1.1 broadcast_select_fusion
  287.6 108.0 %all-reduce.13.cloned.1.call-done = f32[512,512]{1,0:T(8,128)} async-done(((f32[512,512]{1,0:T(8,128)}), f32[512,512]{1,0:T(8,128)}) %all-reduce.13.cloned.1.call-update) | async-done | bytes 1048592 | tf_op jit(solution)/shard_map/psum | solution.py:11
  395.6 1.5 select_bitcast_fusion.3
  397.0 1.5 pad_maximum_fusion.1
  398.6 1.2 copy-done.3
  399.8 1.0 copy.17
  400.8 4.5 conditional.10
  400.8 4.5 convolution_subtract_fusion.2
  405.3 0.9 fusion.29
  406.2 53.0 %all-reduce.15.cloned.1.call-done = f32[2,512,512]{2,1,0:T(8,128)} async-done(((f32[2,512,512]{2,1,0:T(8,128)}), f32[2,512,512]{2,1,0:T(8,128)}) %all-reduce.15.cloned.1.call-update) | async-done | bytes 2097168 | tf_op jit(solution)/shard_map/psum | solution.py:59
  459.2 4.6 conditional.11
  459.4 4.4 convolution_subtract_fusion.3
  463.8 2.3 select_bitcast_fusion
  466.1 3.4 conditional.9
  466.1 3.4 convolution_subtract_fusion.1
  469.6 1.1 copy-done.2
  470.9 2.9 copy.10
  (34 shorter events, 2.0 us)
Async XLA Ops:
  7.2 59.8 %all-reduce.7.cloned.1.call-start = ((), (), s32[]{:S(2)}) async-start(), calls=%async_computation | async-start | bytes 2097152 | tf_op jit(solution)/shard_map/psum | solution.py:11
  12.2 1.2 copy-start.5
  14.7 116.1 %all-reduce.9.cloned.1.call-start = ((), (), s32[]{:S(2)}) async-start(), calls=%async_computation.1 | async-start | bytes 4194304 | tf_op jit(solution)/shard_map/psum | solution.py:34
  69.9 60.9 %copy-start = (f32[512,512]{1,0:T(8,128)S(1)}, f32[512,512]{1,0:T(8,128)}, u32[]{:S(2)}) copy-start(f32[512,512]{1,0:T(8,128)} %all-reduce.7.cloned.1.call-done) | copy-start | bytes 3145732
  69.9 215.4 %all-reduce.11.cloned.1.call-start = ((), (), s32[]{:S(2)}) async-start(), calls=%async_computation.2 | async-start | bytes 2097152 | tf_op jit(solution)/shard_map/psum | solution.py:11
  140.1 1.0 copy-start.4
  229.2 166.3 %all-reduce.13.cloned.1.call-start = ((), (), s32[]{:S(2)}) async-start(), calls=%async_computation.3 | async-start | bytes 2097152 | tf_op jit(solution)/shard_map/psum | solution.py:11
  287.5 171.6 %all-reduce.15.cloned.1.call-start = ((), (), s32[]{:S(2)}) async-start(), calls=%async_computation.4 | async-start | bytes 4194304 | tf_op jit(solution)/shard_map/psum | solution.py:59
  398.5 1.2 copy-start.3
  400.8 4.5 copy-start.1
  469.4 1.2 copy-start.2
Sparse Core Ops, SparseCore 0:
  14.8 52.1 all-reduce.6
  70.8 59.9 all-reduce.8
  229.4 55.9 all-reduce.10
  288.1 107.3 all-reduce.12
  399.2 59.9 all-reduce.14
where the time goes:
time: 487 us; the launch traced here: 481 us
  waiting for transfers between devices  330 us (68%)
  other arithmetic  93.9 us (19%)
  matrix products  21 us (4%)
  local copies, waits for them, and re-layouts  17.7 us (4%)
  between operations  16.8 us (3%)
    psum x3, waiting for transfers between devices, broadcast(): return lax.psum(jnp.where(mine, array, jnp.zeros_like(array)), axis)  216 us
    another operation x14, other arithmetic, local(): jnp.linalg.cholesky(jnp.where(is_owner, block_tiles[0], identity))  78.8 us
    psum x1, waiting for transfers between devices, local(): summed_first = lax.psum(slot_tiles, 'row')  60.8 us
    psum x1, waiting for transfers between devices, local(): summed_second = lax.psum(slot_second, 'row')  53 us
    dot_general x4, matrix products, outer_product(): lax.dot_general(left, right, (((1,), (1,)), ((), ())), precision=highest,...  15.6 us
  transfers between devices with their start and end apart: 5, of which 5 were waited for; matrix products, arithmetic and copies ran while one was open for 1% of the time, Pallas kernels for 0%

commit v1 on v0

--- a/solution.py
+++ b/solution.py
@@ -56,7 +56,11 @@
     local_second = lax.cond(col_index == 1, solve_panel, lambda: zero_tile)
     own_second = broadcast(local_second, "col", 1)
     slot_second = jnp.stack([jnp.where(row_index == column, own_second, 0.0) for column in columns])
-    summed_second = lax.psum(slot_second, "row")
+    summed_second = slot_second
+    for hop in (1, 2, 4):
+        summed_second = summed_second + lax.ppermute(
+            summed_second, "row", [(dev, dev ^ hop) for dev in range(8)]
+        )
     remote_second = [summed_second[position] for position in range(cycles)]
     block_tiles = [
         lower_update(

time: 487 us -> 528 us (1.084)
  waiting for transfers between devices: 330 us -> 369 us
    ppermute x0 -> x3, waiting for transfers between devices: none -> 91.3 us  [local(): lax.ppermute(summed_second, 'row', [(dev, dev ^ hop) for dev in range(8)])]
    psum x1 -> x0, waiting for transfers between devices: 53 us -> none  [local(): summed_second = lax.psum(slot_second, 'row')]
    add x0 -> x3, other arithmetic: none -> 6.57 us  [local(): summed_second + lax.ppermute(summed_second, 'row', [(dev, dev ^ hop) for...]
  transfers between devices with their start and end apart: 5 -> 7, of which waited for: 5 -> 7; matrix products, arithmetic and copies ran while one was open for 1% -> 1% of each run, Pallas kernels for 0% -> 0%
where the time goes in v1:
time: 528 us; the launch traced here: 522 us
  waiting for transfers between devices  369 us (70%)
  other arithmetic  98.2 us (19%)
  matrix products  20 us (4%)
  between operations  16.8 us (3%)
  local copies, waits for them, and re-layouts  16.5 us (3%)
    psum x3, waiting for transfers between devices, broadcast(): return lax.psum(jnp.where(mine, array, jnp.zeros_like(array)), axis)  217 us
    ppermute x3, waiting for transfers between devices, local(): lax.ppermute(summed_second, 'row', [(dev, dev ^ hop) for dev in range(8)])  91.3 us
    another operation x14, other arithmetic, local(): jnp.linalg.cholesky(jnp.where(is_owner, block_tiles[0], identity))  79 us
    psum x1, waiting for transfers between devices, local(): summed_first = lax.psum(slot_tiles, 'row')  60.8 us
    dot_general x4, matrix products, outer_product(): lax.dot_general(left, right, (((1,), (1,)), ((), ())), precision=highest,...  14.6 us
  transfers between devices with their start and end apart: 7, of which 7 were waited for; matrix products, arithmetic and copies ran while one was open for 1% of the time, Pallas kernels for 0%

profile of v1, /device:TPU:22, one launch (start us, length us, event | category | flops | bytes accessed | tf_op | source)
XLA Modules:
  0.0 522.2 jit_solution(10872272228777983263)
XLA Ops:
  7.2 5.0 fusion.43
  12.3 1.2 copy-done.6
  13.6 1.1 broadcast_select_fusion.1
  14.7 52.3 %all-reduce.6.cloned.1.call-done = f32[512,512]{1,0:T(8,128)} async-done(((f32[512,512]{1,0:T(8,128)}), f32[512,512]{1,0:T(8,128)}) %all-reduce.6.cloned.1.call-update) | async-done | bytes 1048592 | tf_op jit(solution)/shard_map/psum | solution.py:11
  67.0 1.4 select_bitcast_fusion.5
  68.3 1.5 pad_maximum_fusion
  70.0 60.8 %all-reduce.8.cloned.1.call-done = f32[2,512,512]{2,1,0:T(8,128)} async-done(((f32[2,512,512]{2,1,0:T(8,128)}), f32[2,512,512]{2,1,0:T(8,128)}) %all-reduce.8.cloned.1.call-update) | async-done | bytes 2097168 | tf_op jit(solution)/shard_map/psum | solution.py:34
  130.8 3.5 conditional.7
  130.8 3.4 convolution_subtract_fusion
  134.6 1.1 convert_select_fusion
  135.7 2.5 copy.7
  138.3 1.5 fusion.28
  139.8 1.0 copy-done.5
  140.7 11.7 %cholesky.103 = f32[128,128]{1,0:T(8,128)S(1)} custom-call(f32[128,128]{1,0:T(8,128)S(1)} %cholesky.263), custom_call_target="Cholesky" | custom-call | tf_op jit(solution)/shard_map/jit(cholesky)/cholesky | solution.py:49
  152.5 9.8 %custom-call.31 = f32[1,128,128]{1,2,0:T(8,128)S(1)} custom-call(f32[1,128,128]{2,1,0:T(8,128)S(1)} %get-tuple-element.121), custom_call_target="InvertDiagBlocksLowerTriangular" | custom-call | tf_op jit(solution)/shard_map/jit(cholesky)/cholesky | solution.py:49
  162.4 1.2 constant_dynamic-update-slice_fusion.1
  163.7 1.3 convolution_subtract_fusion.7
  165.0 11.7 %cholesky.215 = f32[128,128]{1,0:T(8,128)S(1)} custom-call(f32[128,128]{1,0:T(8,128)S(1)} %cholesky.267), custom_call_target="Cholesky" | custom-call | tf_op jit(solution)/shard_map/jit(cholesky)/cholesky | solution.py:49
  176.7 10.0 %custom-call.32 = f32[1,128,128]{1,2,0:T(8,128)S(1)} custom-call(f32[1,128,128]{2,1,0:T(8,128)S(1)} %get-tuple-element.118), custom_call_target="InvertDiagBlocksLowerTriangular" | custom-call | tf_op jit(solution)/shard_map/jit(cholesky)/cholesky | solution.py:49
  187.0 1.3 convolution_subtract_fusion.8
  188.3 11.7 %cholesky.236 = f32[128,128]{1,0:T(8,128)S(1)} custom-call(f32[128,128]{1,0:T(8,128)S(1)} %cholesky.272), custom_call_target="Cholesky" | custom-call | tf_op jit(solution)/shard_map/jit(cholesky)/cholesky | solution.py:49
  200.7 9.8 %custom-call.33 = f32[1,128,128]{1,2,0:T(8,128)S(1)} custom-call(f32[1,128,128]{2,1,0:T(8,128)S(1)} %get-tuple-element.115), custom_call_target="InvertDiagBlocksLowerTriangular" | custom-call | tf_op jit(solution)/shard_map/jit(cholesky)/cholesky | solution.py:49
  210.7 1.2 convolution_subtract_fusion.9
  211.9 12.1 %cholesky.253 = f32[128,128]{1,0:T(8,128)S(1)} custom-call(f32[128,128]{1,0:T(8,128)S(1)} %convolution_subtract_fusion.9), custom_call_target="Cholesky" | custom-call | tf_op jit(solution)/shard_map/jit(cholesky)/cholesky | solution.py:49
  224.1 0.7 compare_reduce_fusion
  227.9 1.1 select_select_fusion
  229.1 56.0 %all-reduce.10.cloned.1.call-done = f32[512,512]{1,0:T(8,128)} async-done(((f32[512,512]{1,0:T(8,128)}), f32[512,512]{1,0:T(8,128)}) %all-reduce.10.cloned.1.call-update) | async-done | bytes 1048592 | tf_op jit(solution)/shard_map/psum | solution.py:11
  285.2 1.1 conditional.8
  285.2 1.1 broadcast.194.clone
  286.3 1.1 broadcast_select_fusion
  287.4 108.5 %all-reduce.12.cloned.1.call-done = f32[512,512]{1,0:T(8,128)} async-done(((f32[512,512]{1,0:T(8,128)}), f32[512,512]{1,0:T(8,128)}) %all-reduce.12.cloned.1.call-update) | async-done | bytes 1048592 | tf_op jit(solution)/shard_map/psum | solution.py:11
  395.9 1.5 select_bitcast_fusion.3
  397.7 4.1 collective-permute-done
  403.0 47.1 %collective-permute-done.1 = f32[2,512,512]{2,1,0:T(8,128)S(1)} collective-permute-done((f32[2,512,512]{2,1,0:T(8,128)S(1)}, f32[2,512,512]{2,1,0:T(8,128)S(1)}, u32[]{:S(2)}, u32[]{:S(2)}) %collective-permute-start.1) | collective-permute-done | bytes 2097184 | tf_op jit(solution)/shard_map/ppermute | solution.py:61
  450.1 2.1 fusion.56
  452.7 1.0 copy.17
  453.7 4.6 conditional.10
  453.7 4.4 convolution_subtract_fusion.2
  458.4 0.9 fusion.29
  459.3 40.0 %collective-permute-done.2 = f32[2,512,512]{2,1,0:T(8,128)} collective-permute-done((f32[2,512,512]{2,1,0:T(8,128)}, f32[2,512,512]{2,1,0:T(8,128)}, u32[]{:S(2)}, u32[]{:S(2)}) %collective-permute-start.2) | collective-permute-done | bytes 2097184 | tf_op jit(solution)/shard_map/ppermute | solution.py:61
  499.3 4.0 add.65
  503.3 3.4 conditional.11
  503.3 3.4 convolution_subtract_fusion.3
  506.7 1.1 select_bitcast_fusion
  507.7 3.4 conditional.9
  507.7 3.4 convolution_subtract_fusion.1
  511.2 1.1 copy-done.3
  512.6 2.9 copy.10
  (42 shorter events, 5.1 us)
Async XLA Ops:
  7.2 59.8 %all-reduce.6.cloned.1.call-start = ((), (), s32[]{:S(2)}) async-start(), calls=%async_computation | async-start | bytes 2097152 | tf_op jit(solution)/shard_map/psum | solution.py:11
  12.2 1.2 copy-start.6
  14.6 116.1 %all-reduce.8.cloned.1.call-start = ((), (), s32[]{:S(2)}) async-start(), calls=%async_computation.1 | async-start | bytes 4194304 | tf_op jit(solution)/shard_map/psum | solution.py:34
  69.9 60.9 %copy-start = (f32[512,512]{1,0:T(8,128)S(1)}, f32[512,512]{1,0:T(8,128)}, u32[]{:S(2)}) copy-start(f32[512,512]{1,0:T(8,128)} %all-reduce.6.cloned.1.call-done) | copy-start | bytes 3145732
  69.9 215.3 %all-reduce.10.cloned.1.call-start = ((), (), s32[]{:S(2)}) async-start(), calls=%async_computation.2 | async-start | bytes 2097152 | tf_op jit(solution)/shard_map/psum | solution.py:11
  139.8 1.0 copy-start.5
  229.1 166.8 %all-reduce.12.cloned.1.call-start = ((), (), s32[]{:S(2)}) async-start(), calls=%async_computation.3 | async-start | bytes 2097152 | tf_op jit(solution)/shard_map/psum | solution.py:11
  397.6 4.2 collective-permute-start
  402.3 50.4 %copy-start.4 = (f32[512,1,512]{2,1,0:T(1,128)S(1)}, f32[512,1,512]{2,1,0:T(1,128)}, u32[]{:S(2)}) copy-start(f32[512,1,512]{2,1,0:T(1,128)} %get-tuple-element.106) | copy-start | bytes 3145732
  402.3 47.7 %collective-permute-start.1 = (f32[2,512,512]{2,1,0:T(8,128)S(1)}, f32[2,512,512]{2,1,0:T(8,128)S(1)}, u32[]{:S(2)}, u32[]{:S(2)}) collective-permute-start(f32[2,512,512]{2,1,0:T(8,128)S(1)} %fusion.41), channel_id=1, source_target_pairs={{0,8},{4,12},{8,0},{12,4},{16,24},{20,28},{24,16},{28,20},{1,9},{5... | collective-permute-start | bytes 6291464 | tf_op jit(solution)/shard_map/ppermute | solution.py:61
  452.2 47.1 %collective-permute-start.2 = (f32[2,512,512]{2,1,0:T(8,128)}, f32[2,512,512]{2,1,0:T(8,128)}, u32[]{:S(2)}, u32[]{:S(2)}) collective-permute-start(f32[2,512,512]{2,1,0:T(8,128)} %fusion.56), channel_id=1, source_target_pairs={{0,16},{4,20},{8,24},{12,28},{16,0},{20,4},{24,8},{28,12},{1,17},{... | collective-permute-start | bytes 6291464 | tf_op jit(solution)/shard_map/ppermute | solution.py:61
  453.7 4.6 copy-start.1
  459.3 44.0 %copy-start.2 = (f32[512,512]{1,0:T(8,128)S(1)}, f32[512,512]{1,0:T(8,128)}, u32[]{:S(2)}) copy-start(f32[512,512]{1,0:T(8,128)} %get-tuple-element.175) | copy-start | bytes 3145732
  511.1 1.2 copy-start.3
Sparse Core Ops, SparseCore 0:
  14.8 52.1 all-reduce.5
  70.8 59.9 all-reduce.7
  229.2 55.9 all-reduce.9
  288.0 107.8 all-reduce.11
